TPU v7x, 32 devices: a whole 2x2x4 slice. The times are simulated.
32 devices in a mesh: frames: 4 (over y, core), bricks: 8 (over z, x).
Axes of the slice: x: 2, y: 2, z: 4, core: 2. Of those that a mesh axis runs over, the one named last changes fastest.
Arguments:
- positions: float32 [3, 8, 16384], P(None, 'frames', 'bricks'), may hold values from 0 to 1
- counts: int32 [8, 8], P('frames'), may hold values from 1 to 2048, as said below
- kvec_x: int32 [128], replicated, may hold values from 1 to 64
- kvec_y: int32 [128], replicated, may hold values from 1 to 64
- kvec_z: int32 [8], replicated, may hold values from 1 to 64
Outputs:
- spectrum: float32 [128, 128, 8, 128], P('bricks', 'frames')
Inputs may be any that keep to these rules, and one draw needn't show every extreme that they name: `counts`: in every frame one brick holds exactly 2048 live atoms; the others hold 1 to 2048.
All inputs are finite; a program needn't handle non-finite values.
Results may differ from a plain program's by a relative error of at most 0.0033.
Values sent between devices are 32-bit elements; how exact they have to be, the bound alone decides.
No kernel may reach another device: no remote copies, remote signals or barrier semaphores. Data moves between devices by JAX's collectives and lax.ppermute only.
A program may use at most 64 MiB of HBM per device.

v0:
```python
import functools
import math

import jax
import jax.numpy as jnp
import numpy as np
from jax import lax
from jax.experimental import pallas as pl
from jax.experimental.pallas import tpu as pltpu
from jax.sharding import PartitionSpec as P

NW = 128
KMAX = 64
LANES = 128
UNIT = 4
BIG = 4

def _fit(fun, degree):
    nodes = 0.125 * (1.0 + np.cos(np.pi * (np.arange(64) + 0.5) / 64))
    series = np.polynomial.chebyshev.Chebyshev.fit(nodes, fun(np.sqrt(nodes)), degree, domain=[0.0, 0.25])
    return [float(c) for c in series.convert(kind=np.polynomial.Polynomial).coef]


COS_C = _fit(lambda f: math.sqrt(2.0) * np.cos(np.pi * f), 4)
SIN_C = _fit(lambda f: math.sqrt(2.0) * np.sin(np.pi * f) / f, 4)


def _poly(coefs, u):
    acc = coefs[-1] * u + coefs[-2]
    for c in coefs[-3::-1]:
        acc = acc * u + c
    return acc


def cis(turns):
    f = turns - jnp.round(turns)
    u = f * f
    half_c = _poly(COS_C, u)
    half_s = _poly(SIN_C, u) * f
    return 1.0 - half_s * half_s, half_s * half_c


def density_kernel(ids, first, last, groups, n_x, n_z, share, *refs):
    ints_ref, pos_ref = refs[:2]
    prod_in, kb_ref = (None, refs[3]) if first else refs[2:4]
    outs = refs[2:-2] if first else refs[4:-2]
    left_ref, right_ref = refs[-2:]
    rows = n_x * n_z
    n_shards, _, frames_here, capacity = pos_ref.shape
    bricks = lax.axis_size("bricks")
    brick = lax.axis_index("bricks")
    lane = lax.broadcasted_iota(jnp.int32, (n_z, LANES), 1)
    at_x = frames_here * bricks
    at_z = at_x + n_x * bricks
    at_y = at_z + n_z

    if first:
        for row in range(n_x + n_z + 16):
            if row < n_x:
                k = ints_ref[at_x + brick * n_x + row].astype(jnp.float32)
            elif row < n_x + n_z:
                k = ints_ref[at_z + row - n_x].astype(jnp.float32)
            else:
                q = row - n_x - n_z
                k = float(q + 1 if q < 8 else 8 * (q - 7))
            kb_ref[row : row + 1, :] = jnp.full((1, LANES), k, jnp.float32)

    for frame in range(frames_here):
        counts = [ints_ref[frame * bricks + (brick ^ d)] for d in ids]
        starts = [jnp.int32(0)]
        for count in counts:
            starts.append(starts[-1] + (count + LANES - 1) // LANES)

        def build(item, frame=frame, counts=counts, starts=starts):
            shard, start, count = jnp.int32(0), starts[0], counts[0]
            for s in range(1, n_shards):
                later = item >= starts[s]
                shard = jnp.where(later, s, shard)
                start = jnp.where(later, starts[s], start)
                count = jnp.where(later, counts[s], count)
            offset = (item - start) * LANES
            where = pl.ds(pl.multiple_of(jnp.minimum(offset, capacity - LANES), LANES), LANES)
            x = pos_ref[shard, 0, pl.ds(frame, 1), where]
            y = pos_ref[shard, 1, pl.ds(frame, 1), where]
            z = pos_ref[shard, 2, pl.ds(frame, 1), where]
            cx, sx = cis(kb_ref[0:n_x, :] * x)
            cz, sz = cis(kb_ref[n_x : n_x + n_z, :] * z)
            cy, sy = cis(kb_ref[n_x + n_z : n_x + n_z + 16, :] * y)
            live = lane + offset < count
            cz = jnp.where(live, cz, 0.0)
            sz = jnp.where(live, sz, 0.0)
            to = pl.ds(pl.multiple_of(item * LANES, LANES), LANES)
            for i in range(0, n_x, 2):
                re, im = [], []
                for q in (i, i + 1):
                    a, b = cx[q : q + 1], sx[q : q + 1]
                    re.append(a * cz - b * sz)
                    im.append(b * cz + a * sz)
                at = i * n_z
                left_ref[at : at + 2 * n_z, to] = jnp.concatenate(re, axis=0).astype(jnp.bfloat16)
                at += rows
                left_ref[at : at + 2 * n_z, to] = jnp.concatenate(im, axis=0).astype(jnp.bfloat16)
            ce, se = cy[0:8], sy[0:8]
            re, im = [ce], [se]
            for q in range(8, 15):
                a, b = cy[q : q + 1], sy[q : q + 1]
                re.append(a * ce - b * se)
                im.append(b * ce + a * se)
            for q in range(0, 8, 2):
                right_ref[8 * q : 8 * q + 16, to] = jnp.concatenate(re[q : q + 2], axis=0).astype(jnp.bfloat16)
                right_ref[KMAX + 8 * q : KMAX + 8 * q + 16, to] = jnp.concatenate(im[q : q + 2], axis=0).astype(jnp.bfloat16)

        def build_unit(unit, carry, build=build):
            for g in range(UNIT):
                build(unit * UNIT + g)
            return carry

        units = (starts[-1] + UNIT - 1) // UNIT
        lax.fori_loop(0, units, build_unit, 0)
        prod_ref = outs[0].at[frame] if not last else outs[-1].at[frame]
        prod_ref[...] = jnp.zeros(prod_ref.shape, jnp.float32) if first else prod_in[frame]

        def multiply(width):
            def step(base):
                where = pl.ds(pl.multiple_of(base, UNIT * LANES), width)
                prod_ref[...] += lax.dot_general(
                    left_ref[:, where],
                    right_ref[:, where],
                    (((1,), (1,)), ((), ())),
                    preferred_element_type=jnp.float32,
                )

            return step

        wide = multiply(BIG * UNIT * LANES)
        full = units // BIG

        def wide_step(i, carry, wide=wide):
            wide(i * (BIG * UNIT * LANES))
            return carry

        lax.fori_loop(0, full, wide_step, 0)
        for rest in range(1, BIG):

            @pl.when(units - full * BIG == rest)
            def _(rest=rest, multiply=multiply, full=full):
                multiply(rest * UNIT * LANES)(full * (BIG * UNIT * LANES))

    if last:
        send_own_rows(outs, groups, rows, share, frames_here, ints_ref, at_y)


def send_own_rows(outs, groups, rows, share, frames_here, ints_ref, at_y):
    prods = outs[-1]
    width = groups * share
    group = lax.axis_index("frames")
    column = lax.broadcasted_iota(jnp.int32, (1, width), 1)
    wanted = jnp.zeros((1, width), jnp.int32)
    for dest in range(groups):
        base = at_y + (group ^ dest) * share
        for j in range(share):
            wanted = jnp.where(column == dest * share + j, ints_ref[base + j], wanted)
    ks = lax.broadcasted_iota(jnp.int32, (KMAX, width), 0) + 1
    hot = jnp.where(ks == wanted, 1.0, 0.0).astype(jnp.bfloat16)
    none = jnp.zeros_like(hot)
    hot = jnp.concatenate(
        [jnp.concatenate([hot, none], axis=1), jnp.concatenate([none, hot], axis=1)], axis=0
    )
    hot = jnp.concatenate([hot, hot, hot], axis=0)
    first_half = lax.broadcasted_iota(jnp.int32, (rows, 2 * KMAX), 1) < KMAX
    for frame in range(frames_here):
        top = prods[frame, 0:rows, :]
        low = pltpu.roll(prods[frame, rows : 2 * rows, :], KMAX, 1)
        terms = jnp.where(first_half, top - low, -(top + low))
        hi = terms.astype(jnp.bfloat16)
        rest = terms - hi.astype(jnp.float32)
        mid = rest.astype(jnp.bfloat16)
        tail = (rest - mid.astype(jnp.float32)).astype(jnp.bfloat16)
        split = jnp.concatenate([hi, mid, tail], axis=1)
        picked = lax.dot_general(
            hot, split, (((0,), (1,)), ((), ())), preferred_element_type=jnp.float32
        )
        for part in range(2):
            for dest in range(groups):
                at = part * width + dest * share
                to = (frame * 2 + part) * share
                outs[dest][to : to + share, :] = picked[at : at + share, :]


def dft_table(table_ref, frames_total, atoms):
    weights = [0.5 - 0.5 * math.cos(2.0 * math.pi * (t + 0.5) / frames_total) for t in range(frames_total)]
    scale = 1.0 / math.sqrt(atoms * sum(w * w for w in weights))
    shape = (2 * frames_total, NW)
    row = lax.broadcasted_iota(jnp.int32, shape, 0)
    time = row // 2
    real = row % 2 == 0
    freq = lax.broadcasted_iota(jnp.int32, shape, 1)
    window = 0.5 - 0.5 * cis((time.astype(jnp.float32) + 0.5) / frames_total)[0]
    c, s = cis((time * freq % NW).astype(jnp.float32) / NW)
    cw, sw = scale * window * c, scale * window * s
    full = jnp.concatenate([jnp.where(real, cw, sw), jnp.where(real, -sw, cw)], axis=1)
    hi = full.astype(jnp.bfloat16)
    lo = (full - hi.astype(jnp.float32)).astype(jnp.bfloat16)
    none = jnp.zeros_like(hi)
    size = 2 * frames_total
    for split, part in enumerate((hi, lo, hi)):
        at = split * 2 * size
        table_ref[at : at + size, :] = jnp.concatenate([part, none], axis=1)
        table_ref[at + size : at + 2 * size, :] = jnp.concatenate([none, part], axis=1)


def spectrum_kernel(groups, share, chunk, n_x, n_z, frames_total, atoms, *refs):
    srcs = refs[:groups]
    out_ref, all_ref, table_ref = refs[groups:]
    block = srcs[0].shape[0]
    terms = groups * block // share

    @pl.when(pl.program_id(0) == 0)
    def _():
        for distance in range(groups):
            at = pl.multiple_of((lax.axis_index("frames") ^ distance) * block, block)
            all_ref[pl.ds(at, block), :] = srcs[distance][...]
        dft_table(table_ref, frames_total, atoms)

    base = pl.program_id(0) * chunk
    for pair in range(chunk // 2):
        j = base + 2 * pair
        x = jnp.concatenate(
            [all_ref[pl.ds(j + q, terms, stride=share), :] for q in range(2)], axis=0
        )
        hi = x.astype(jnp.bfloat16)
        lo = (x - hi.astype(jnp.float32)).astype(jnp.bfloat16)
        y = lax.dot_general(
            jnp.concatenate([hi, hi, lo], axis=0),
            table_ref[...],
            (((0,), (0,)), ((), ())),
            preferred_element_type=jnp.float32,
        )
        for q in range(2):
            re = y[:, 2 * q * NW : (2 * q + 1) * NW]
            im = y[:, (2 * q + 1) * NW : (2 * q + 2) * NW]
            out_ref[:, 2 * pair + q] = (re * re + im * im).reshape(n_x, n_z, NW)


def swap(value, axis, size, distance):
    return lax.ppermute(value, axis, [(i, i ^ distance) for i in range(size)])


def per_device(positions, counts, kvec_x, kvec_y, kvec_z):
    groups = lax.axis_size("frames")
    bricks = lax.axis_size("bricks")
    frames_here, capacity = positions.shape[1], positions.shape[2]
    n_x, n_z = kvec_x.shape[0] // bricks, kvec_z.shape[0]
    rows = n_x * n_z
    share = kvec_y.shape[0] // groups
    block = frames_here * 2 * share
    vmem = pl.BlockSpec(memory_space=pltpu.VMEM)
    smem = pl.BlockSpec(memory_space=pltpu.SMEM)
    prods_shape = (frames_here, 2 * rows, 2 * KMAX)
    waves_shape = (n_x + n_z + 16, LANES)
    ints = jnp.concatenate([counts.reshape(-1), kvec_x, kvec_z, kvec_y])

    def density(shards, ids, sums, last):
        first = sums is None
        lanes = -(-len(ids) * capacity // (BIG * UNIT * LANES)) * BIG * UNIT * LANES
        scratch = [
            pltpu.VMEM((2 * rows, lanes), jnp.bfloat16),
            pltpu.VMEM((2 * KMAX, lanes), jnp.bfloat16),
        ]
        if last:
            out_shape = [jax.ShapeDtypeStruct((block, rows), jnp.float32)] * groups
            scratch = [pltpu.VMEM(prods_shape, jnp.float32)] + scratch
        else:
            out_shape = [jax.ShapeDtypeStruct(prods_shape, jnp.float32)]
            if first:
                out_shape.append(jax.ShapeDtypeStruct(waves_shape, jnp.float32))
        atoms = frames_here * len(ids) * capacity
        return pl.pallas_call(
            functools.partial(density_kernel, ids, first, last, groups, n_x, n_z, share),
            out_shape=out_shape,
            in_specs=[smem] + [vmem] * (1 if first else 3),
            out_specs=[vmem] * len(out_shape),
            scratch_shapes=scratch,
            cost_estimate=pl.CostEstimate(
                flops=atoms * rows * KMAX * 8, bytes_accessed=atoms * 12, transcendentals=0
            ),
            compiler_params=pltpu.CompilerParams(vmem_limit_bytes=48 << 20),
            name="density",
        )(ints, shards, *([] if first else sums))

    held, fresh, ids = positions[None], positions[None], [0]
    new, sums, waves = [0], None, None
    distance = bricks // 2
    while distance:
        got = swap(held, "bricks", bricks, distance)
        out = density(fresh, new, sums, False)
        waves = out[1] if sums is None else waves
        got, prods = lax.optimization_barrier((got, out[0]))
        sums = (prods, waves)
        new = [i ^ distance for i in ids]
        ids, fresh = ids + new, got
        distance //= 2
        if distance:
            held = jnp.concatenate([held, got], axis=0)
    sends = density(fresh, new, sums, True)
    got = [sends[0]] + [swap(sends[d], "frames", groups, d) for d in range(1, groups)]

    chunk = min(8, share)
    frames_total = frames_here * groups
    return pl.pallas_call(
        functools.partial(
            spectrum_kernel, groups, share, chunk, n_x, n_z, frames_total, capacity * bricks
        ),
        out_shape=jax.ShapeDtypeStruct((n_x, share, n_z, NW), jnp.float32),
        grid=(share // chunk,),
        in_specs=[vmem] * groups,
        out_specs=pl.BlockSpec((n_x, chunk, n_z, NW), lambda c: (0, c, 0, 0)),
        scratch_shapes=[
            pltpu.VMEM((groups * block, rows), jnp.float32),
            pltpu.VMEM((12 * frames_total, 4 * NW), jnp.bfloat16),
        ],
        compiler_params=pltpu.CompilerParams(vmem_limit_bytes=16 << 20),
        name="spectrum",
    )(*got)


def solution(mesh):
    return jax.shard_map(
        per_device,
        mesh=mesh,
        in_specs=(P(None, "frames", "bricks"), P("frames", None), P(), P(), P()),
        out_specs=P("bricks", "frames", None, None),
        check_vma=False,
    )
```

profile of v0, /device:TPU:0, one launch (start us, length us, event | category | flops | bytes accessed | tf_op | source)
XLA Modules:
  0.0 39.6 jit_solution(15684494913879286532)
XLA Ops:
  0.0 4.0 %collective-permute-start = (f32[1,3,2,2048]{3,2,1,0:T(2,128)}, f32[1,3,2,2048]{3,2,1,0:T(2,128)S(1)}, u32[]{:S(2)}, u32[]{:S(2)}) collective-permute-start(f32[1,3,2,2048]{3,2,1,0:T(2,128)} %bitcast.1), channel_id=1, source_target_pairs={{0,4},{1,5},{2,6},{3,7},{4,0},{5,1},{6,2},{7,3},{8,12},{9,13},{10,... | collective-permute-start | bytes 147464 | tf_op jit(solution)/shard_map/ppermute | solution.py:246
  4.0 0.8 %reshape.3 = s32[16]{0:T(128)S(1)} reshape(s32[2,8]{1,0:T(2,128)} %param.6) | data formatting | bytes 128 | tf_op jit(solution)/shard_map/reshape | solution.py:261
  4.8 0.8 %pad_add_fusion.refs_0_ = s32[280]{0:T(512)S(1)} fusion(s32[128]{0:T(128)} %param.8, s32[8]{0:T(128)} %param.9, s32[128]{0:T(128)} %param.7, s32[16]{0:T(128)S(1)} %reshape.3), kind=kLoop, calls=%fused_computation.2 | loop fusion | flops 840 | bytes 2240 | tf_op jit(solution)/shard_map/concatenate | solution.py:261
  5.6 0.0 copy-start
  5.6 0.8 %copy-done = f32[3,2,2048]{2,1,0:T(2,128)S(1)} copy-done((f32[3,2,2048]{2,1,0:T(2,128)S(1)}, f32[3,2,2048]{2,1,0:T(2,128)}, u32[]{:S(2)}) %copy-start) | copy-done | bytes 49176
  6.4 0.0 copy-start.1
  6.4 2.8 %density.4 = (f32[2,256,128]{2,1,0:T(8,128)S(1)}, f32[40,128]{1,0:T(8,128)S(1)}) custom-call(s32[280]{0:T(512)S(1)} %pad_add_fusion.refs_0_, f32[1,3,2,2048]{3,2,1,0:T(2,128)S(1)} %bitcast.2), custom_call_target="tpu_custom_call" | custom-call | flops 268435456 | bytes 49152 | tf_op jit(solution)/shard_map/density/pallas_call | solution.py:278
  9.2 0.0 collective-permute-done.refs_1_
  9.3 2.3 %collective-permute-start.1 = (f32[2,3,2,2048]{3,2,1,0:T(2,128)S(1)}, f32[2,3,2,2048]{3,2,1,0:T(2,128)S(1)}, u32[]{:S(2)}, u32[]{:S(2)}) collective-permute-start(f32[2,3,2,2048]{3,2,1,0:T(2,128)S(1)} %pad_maximum_fusion.1), channel_id=1, source_target_pairs={{0,2},{1,3},{2,0},{3,1},{4,6},{5,7},{6,4},{7,5},{8,10},{9,11},{10,... | collective-permute-start | bytes 294920 | tf_op jit(solution)/shard_map/ppermute | solution.py:246
  11.6 2.5 %density.5.refs_2_ = f32[2,256,128]{2,1,0:T(8,128)S(1)} custom-call(s32[280]{0:T(512)S(1)} %pad_add_fusion.refs_0_, f32[1,3,2,2048]{3,2,1,0:T(2,128)S(1)} %collective-permute-done.refs_1_, f32[2,256,128]{2,1,0:T(8,128)S(1)} %get-tuple-element.19.refs_2_, f32[40,128]{1,0:T(8,128)S(1)} %get-tuple-element.20.refs_3_), custom_call_target="tpu_custom_call" | custom-call | flops 268435456 | bytes 49152 | tf_op jit(solution)/shard_map/density/pallas_call | solution.py:278
  14.1 0.1 collective-permute-done.1.refs_1_
  14.2 0.0 copy-done.1
  14.2 0.1 pad_maximum_fusion
  14.3 1.0 %collective-permute-start.2 = (f32[4,3,2,2048]{3,2,1,0:T(2,128)S(1)}, f32[4,3,2,2048]{3,2,1,0:T(2,128)S(1)}, u32[]{:S(2)}, u32[]{:S(2)}) collective-permute-start(f32[4,3,2,2048]{3,2,1,0:T(2,128)S(1)} %pad_maximum_fusion), channel_id=1, source_target_pairs={{0,1},{1,0},{2,3},{3,2},{4,5},{5,4},{6,7},{7,6},{8,9},{9,8},{10,11... | collective-permute-start | bytes 589832 | tf_op jit(solution)/shard_map/ppermute | solution.py:246
  15.3 5.0 %density.6.refs_2_ = f32[2,256,128]{2,1,0:T(8,128)S(1)} custom-call(s32[280]{0:T(512)S(1)} %pad_add_fusion.refs_0_, f32[2,3,2,2048]{3,2,1,0:T(2,128)S(1)} %collective-permute-done.1.refs_1_, f32[2,256,128]{2,1,0:T(8,128)S(1)} %density.5.refs_2_, f32[40,128]{1,0:T(8,128)S(1)} %get-tuple-element.20.refs_3_), custom_call_target="tpu_custom_call" | custom-call | flops 536870912 | bytes 98304 | tf_op jit(solution)/shard_map/density/pallas_call | solution.py:278
  20.3 0.1 collective-permute-done.2.refs_1_
  20.4 7.6 %density.7 = (f32[128,128]{1,0:T(8,128)S(1)}, f32[128,128]{1,0:T(8,128)S(1)}, f32[128,128]{1,0:T(8,128)S(1)}, f32[128,128]{1,0:T(8,128)S(1)}) custom-call(s32[280]{0:T(512)S(1)} %pad_add_fusion.refs_0_, f32[4,3,2,2048]{3,2,1,0:T(2,128)S(1)} %collective-permute-done.2.refs_1_, f32[2,256,128]{2,1,0:T(8,128)S(1)} %density.6.refs_2_, ...), custom_call_target="tpu_custom_call" | custom-call | flops 1073741824 | bytes 196608 | tf_op jit(solution)/shard_map/density/pallas_call | solution.py:278
  28.0 0.1 collective-permute-start.3
  28.1 4.8 %collective-permute-start.4 = (f32[128,128]{1,0:T(8,128)S(1)}, f32[128,128]{1,0:T(8,128)S(1)}, u32[]{:S(2)}, u32[]{:S(2)}) collective-permute-start(f32[128,128]{1,0:T(8,128)S(1)} %get-tuple-element.27), channel_id=1, source_target_pairs={{0,16},{8,24},{16,0},{24,8},{1,17},{9,25},{17,1},{25,9},{2,18},{10... | collective-permute-start | bytes 196616 | tf_op jit(solution)/shard_map/ppermute | solution.py:246
  32.9 0.1 collective-permute-start.5
  32.9 0.0 collective-permute-done.3.refs_1_
  32.9 2.6 %collective-permute-done.4.refs_2_ = f32[128,128]{1,0:T(8,128)S(1)} collective-permute-done((f32[128,128]{1,0:T(8,128)S(1)}, f32[128,128]{1,0:T(8,128)S(1)}, u32[]{:S(2)}, u32[]{:S(2)}) %collective-permute-start.4) | collective-permute-done | bytes 65568 | tf_op jit(solution)/shard_map/ppermute | solution.py:246
  35.5 1.4 %collective-permute-done.5.refs_3_ = f32[128,128]{1,0:T(8,128)S(1)} collective-permute-done((f32[128,128]{1,0:T(8,128)S(1)}, f32[128,128]{1,0:T(8,128)S(1)}, u32[]{:S(2)}, u32[]{:S(2)}) %collective-permute-start.5) | collective-permute-done | bytes 65568 | tf_op jit(solution)/shard_map/ppermute | solution.py:246
  36.9 2.7 %spectrum.1 = f32[16,32,8,128]{3,2,1,0:T(8,128)} custom-call(f32[128,128]{1,0:T(8,128)S(1)} %get-tuple-element.25.refs_0_, f32[128,128]{1,0:T(8,128)S(1)} %collective-permute-done.3.refs_1_, f32[128,128]{1,0:T(8,128)S(1)} %collective-permute-done.4.refs_2_, f32[128,128]{1,0:T(8,128)S(1)} %collective-permute-done.5.refs_3_), custom_call_target="tpu_custom_call" | custom-call | tf_op jit(solution)/shard_map/spectrum/pallas_call | solution.py:310
  (1 shorter events, 0.0 us)
Async XLA Ops:
  0.0 9.2 %collective-permute-start = (f32[1,3,2,2048]{3,2,1,0:T(2,128)}, f32[1,3,2,2048]{3,2,1,0:T(2,128)S(1)}, u32[]{:S(2)}, u32[]{:S(2)}) collective-permute-start(f32[1,3,2,2048]{3,2,1,0:T(2,128)} %bitcast.1), channel_id=1, source_target_pairs={{0,4},{1,5},{2,6},{3,7},{4,0},{5,1},{6,2},{7,3},{8,12},{9,13},{10,... | collective-permute-start | bytes 147464 | tf_op jit(solution)/shard_map/ppermute | solution.py:246
  5.6 0.8 %copy-start = (f32[3,2,2048]{2,1,0:T(2,128)S(1)}, f32[3,2,2048]{2,1,0:T(2,128)}, u32[]{:S(2)}) copy-start(f32[3,2,2048]{2,1,0:T(2,128)} %param.5) | copy-start | bytes 147460
  6.4 7.9 %copy-start.1 = (f32[3,2,2048]{2,1,0:T(2,128)S(1)}, f32[3,2,2048]{2,1,0:T(2,128)}, u32[]{:S(2)}) copy-start(f32[3,2,2048]{2,1,0:T(2,128)} %param.5) | copy-start | bytes 147460
  9.3 5.0 %collective-permute-start.1 = (f32[2,3,2,2048]{3,2,1,0:T(2,128)S(1)}, f32[2,3,2,2048]{3,2,1,0:T(2,128)S(1)}, u32[]{:S(2)}, u32[]{:S(2)}) collective-permute-start(f32[2,3,2,2048]{3,2,1,0:T(2,128)S(1)} %pad_maximum_fusion.1), channel_id=1, source_target_pairs={{0,2},{1,3},{2,0},{3,1},{4,6},{5,7},{6,4},{7,5},{8,10},{9,11},{10,... | collective-permute-start | bytes 294920 | tf_op jit(solution)/shard_map/ppermute | solution.py:246
  14.3 6.0 %collective-permute-start.2 = (f32[4,3,2,2048]{3,2,1,0:T(2,128)S(1)}, f32[4,3,2,2048]{3,2,1,0:T(2,128)S(1)}, u32[]{:S(2)}, u32[]{:S(2)}) collective-permute-start(f32[4,3,2,2048]{3,2,1,0:T(2,128)S(1)} %pad_maximum_fusion), channel_id=1, source_target_pairs={{0,1},{1,0},{2,3},{3,2},{4,5},{5,4},{6,7},{7,6},{8,9},{9,8},{10,11... | collective-permute-start | bytes 589832 | tf_op jit(solution)/shard_map/ppermute | solution.py:246
  28.0 4.9 %collective-permute-start.3 = (f32[128,128]{1,0:T(8,128)S(1)}, f32[128,128]{1,0:T(8,128)S(1)}, u32[]{:S(2)}, u32[]{:S(2)}) collective-permute-start(f32[128,128]{1,0:T(8,128)S(1)} %get-tuple-element.26), channel_id=1, source_target_pairs={{0,8},{8,0},{16,24},{24,16},{1,9},{9,1},{17,25},{25,17},{2,10},{10... | collective-permute-start | bytes 196616 | tf_op jit(solution)/shard_map/ppermute | solution.py:246
  28.1 7.5 %collective-permute-start.4 = (f32[128,128]{1,0:T(8,128)S(1)}, f32[128,128]{1,0:T(8,128)S(1)}, u32[]{:S(2)}, u32[]{:S(2)}) collective-permute-start(f32[128,128]{1,0:T(8,128)S(1)} %get-tuple-element.27), channel_id=1, source_target_pairs={{0,16},{8,24},{16,0},{24,8},{1,17},{9,25},{17,1},{25,9},{2,18},{10... | collective-permute-start | bytes 196616 | tf_op jit(solution)/shard_map/ppermute | solution.py:246
  32.9 4.0 %collective-permute-start.5 = (f32[128,128]{1,0:T(8,128)S(1)}, f32[128,128]{1,0:T(8,128)S(1)}, u32[]{:S(2)}, u32[]{:S(2)}) collective-permute-start(f32[128,128]{1,0:T(8,128)S(1)} %get-tuple-element.28), channel_id=1, source_target_pairs={{0,24},{8,16},{16,8},{24,0},{1,25},{9,17},{17,9},{25,1},{2,26},{10... | collective-permute-start | bytes 196616 | tf_op jit(solution)/shard_map/ppermute | solution.py:246
where the time goes:
time: 40.3 us; the launch traced here: 39.6 us
  Pallas kernels  20.6 us (51%)
  starting transfers between devices  12.2 us (30%)
  waiting for transfers between devices  4.19 us (10%)
  local copies, waits for them, and re-layouts  1.56 us (4%)
  other arithmetic  0.91 us (2%)
    pallas_call x4, Pallas kernels, density(): pl.pallas_call(functools.partial(density_kernel, ids, first, last, groups...  18 us
    ppermute x6, starting transfers between devices, swap(): return lax.ppermute(value, axis, [(i, i ^ distance) for i in range(size)])  12.2 us
    ppermute x6, waiting for transfers between devices, swap(): return lax.ppermute(value, axis, [(i, i ^ distance) for i in range(size)])  4.19 us
    pallas_call x1, Pallas kernels, per_device(): pl.pallas_call(functools.partial(spectrum_kernel, groups, share, chunk, n...  2.66 us
  transfers between devices with their start and end apart: 6, of which 4 were waited for; matrix products, arithmetic and copies ran while one was open for 4% of the time, Pallas kernels for 26%

commit v1 on v0

--- a/solution.py
+++ b/solution.py
@@ -13,7 +13,7 @@
 KMAX = 64
 LANES = 128
 UNIT = 4
-BIG = 4
+BIG = 8
 
 def _fit(fun, degree):
     nodes = 0.125 * (1.0 + np.cos(np.pi * (np.arange(64) + 0.5) / 64))
@@ -41,37 +41,50 @@
 
 
 def density_kernel(ids, first, last, groups, n_x, n_z, share, *refs):
-    ints_ref, pos_ref = refs[:2]
-    prod_in, kb_ref = (None, refs[3]) if first else refs[2:4]
-    outs = refs[2:-2] if first else refs[4:-2]
-    left_ref, right_ref = refs[-2:]
+    n_args = 4 if first else 2 if last else 1
+    args, refs = refs[:n_args], refs[n_args:]
+    left_ref, right_ref, row_ref, arg_sem = refs[-4:]
+    refs = refs[:-4]
+    if not first:
+        (pos_ref, prod_in, kb_ref), refs = refs[:3], refs[3:]
+    local = refs[-n_args:]
+    outs = refs[:-n_args]
+    copies = [
+        pltpu.make_async_copy(args[i], local[i], arg_sem.at[i]) for i in range(n_args)
+    ]
+    for copy in copies:
+        copy.start()
+    counts_ref = local[0]
+    if first:
+        pos_ref, kb_ref = local[3], outs[1]
     rows = n_x * n_z
     n_shards, _, frames_here, capacity = pos_ref.shape
-    bricks = lax.axis_size("bricks")
     brick = lax.axis_index("bricks")
     lane = lax.broadcasted_iota(jnp.int32, (n_z, LANES), 1)
-    at_x = frames_here * bricks
-    at_z = at_x + n_x * bricks
-    at_y = at_z + n_z
-
+
+    copies[0].wait()
     if first:
+        kx_ref, kz_ref = local[1:3]
+        copies[1].wait()
+        copies[2].wait()
         for row in range(n_x + n_z + 16):
             if row < n_x:
-                k = ints_ref[at_x + brick * n_x + row].astype(jnp.float32)
+                k = kx_ref[brick * n_x + row].astype(jnp.float32)
             elif row < n_x + n_z:
-                k = ints_ref[at_z + row - n_x].astype(jnp.float32)
+                k = kz_ref[row - n_x].astype(jnp.float32)
             else:
                 q = row - n_x - n_z
                 k = float(q + 1 if q < 8 else 8 * (q - 7))
             kb_ref[row : row + 1, :] = jnp.full((1, LANES), k, jnp.float32)
+        copies[3].wait()
 
     for frame in range(frames_here):
-        counts = [ints_ref[frame * bricks + (brick ^ d)] for d in ids]
+        counts = [counts_ref[frame, brick ^ d] for d in ids]
         starts = [jnp.int32(0)]
         for count in counts:
             starts.append(starts[-1] + (count + LANES - 1) // LANES)
 
-        def build(item, frame=frame, counts=counts, starts=starts):
+        def build(item, slot, frame=frame, counts=counts, starts=starts):
             shard, start, count = jnp.int32(0), starts[0], counts[0]
             for s in range(1, n_shards):
                 later = item >= starts[s]
@@ -90,10 +103,21 @@
             cz = jnp.where(live, cz, 0.0)
             sz = jnp.where(live, sz, 0.0)
             to = pl.ds(pl.multiple_of(item * LANES, LANES), LANES)
+            half = n_x + 8
+            base = slot * 2 * half
+            row_ref[base : base + half, :] = jnp.concatenate([cx, cy[8:16]], axis=0)
+            row_ref[base + half : base + 2 * half, :] = jnp.concatenate([sx, sy[8:16]], axis=0)
+
+            def spread(q):
+                return (
+                    row_ref[pl.ds(base + q, 8, stride=0), :],
+                    row_ref[pl.ds(base + half + q, 8, stride=0), :],
+                )
+
             for i in range(0, n_x, 2):
                 re, im = [], []
                 for q in (i, i + 1):
-                    a, b = cx[q : q + 1], sx[q : q + 1]
+                    a, b = spread(q)
                     re.append(a * cz - b * sz)
                     im.append(b * cz + a * sz)
                 at = i * n_z
@@ -102,8 +126,8 @@
                 left_ref[at : at + 2 * n_z, to] = jnp.concatenate(im, axis=0).astype(jnp.bfloat16)
             ce, se = cy[0:8], sy[0:8]
             re, im = [ce], [se]
-            for q in range(8, 15):
-                a, b = cy[q : q + 1], sy[q : q + 1]
+            for q in range(7):
+                a, b = spread(n_x + q)
                 re.append(a * ce - b * se)
                 im.append(b * ce + a * se)
             for q in range(0, 8, 2):
@@ -112,7 +136,7 @@
 
         def build_unit(unit, carry, build=build):
             for g in range(UNIT):
-                build(unit * UNIT + g)
+                build(unit * UNIT + g, g)
             return carry
 
         units = (starts[-1] + UNIT - 1) // UNIT
@@ -147,19 +171,20 @@
                 multiply(rest * UNIT * LANES)(full * (BIG * UNIT * LANES))
 
     if last:
-        send_own_rows(outs, groups, rows, share, frames_here, ints_ref, at_y)
-
-
-def send_own_rows(outs, groups, rows, share, frames_here, ints_ref, at_y):
+        copies[1].wait()
+        send_own_rows(outs, groups, rows, share, frames_here, local[1])
+
+
+def send_own_rows(outs, groups, rows, share, frames_here, ky_ref):
     prods = outs[-1]
     width = groups * share
     group = lax.axis_index("frames")
     column = lax.broadcasted_iota(jnp.int32, (1, width), 1)
     wanted = jnp.zeros((1, width), jnp.int32)
     for dest in range(groups):
-        base = at_y + (group ^ dest) * share
+        base = (group ^ dest) * share
         for j in range(share):
-            wanted = jnp.where(column == dest * share + j, ints_ref[base + j], wanted)
+            wanted = jnp.where(column == dest * share + j, ky_ref[base + j], wanted)
     ks = lax.broadcasted_iota(jnp.int32, (KMAX, width), 0) + 1
     hot = jnp.where(ks == wanted, 1.0, 0.0).astype(jnp.bfloat16)
     none = jnp.zeros_like(hot)
@@ -255,17 +280,26 @@
     share = kvec_y.shape[0] // groups
     block = frames_here * 2 * share
     vmem = pl.BlockSpec(memory_space=pltpu.VMEM)
-    smem = pl.BlockSpec(memory_space=pltpu.SMEM)
     prods_shape = (frames_here, 2 * rows, 2 * KMAX)
     waves_shape = (n_x + n_z + 16, LANES)
-    ints = jnp.concatenate([counts.reshape(-1), kvec_x, kvec_z, kvec_y])
+    hbm = pl.BlockSpec(memory_space=pltpu.HBM)
 
     def density(shards, ids, sums, last):
         first = sums is None
         lanes = -(-len(ids) * capacity // (BIG * UNIT * LANES)) * BIG * UNIT * LANES
-        scratch = [
+        args = [counts]
+        if first:
+            args += [kvec_x, kvec_z, shards]
+        elif last:
+            args += [kvec_y]
+        scratch = [pltpu.SMEM(arg.shape, jnp.int32) for arg in args[:3]]
+        if first:
+            scratch.append(pltpu.VMEM(shards.shape, jnp.float32))
+        scratch += [
             pltpu.VMEM((2 * rows, lanes), jnp.bfloat16),
             pltpu.VMEM((2 * KMAX, lanes), jnp.bfloat16),
+            pltpu.VMEM((UNIT * 2 * (n_x + 8), LANES), jnp.float32),
+            pltpu.SemaphoreType.DMA((len(args),)),
         ]
         if last:
             out_shape = [jax.ShapeDtypeStruct((block, rows), jnp.float32)] * groups
@@ -278,7 +312,7 @@
         return pl.pallas_call(
             functools.partial(density_kernel, ids, first, last, groups, n_x, n_z, share),
             out_shape=out_shape,
-            in_specs=[smem] + [vmem] * (1 if first else 3),
+            in_specs=[hbm] * len(args) + [vmem] * (0 if first else 3),
             out_specs=[vmem] * len(out_shape),
             scratch_shapes=scratch,
             cost_estimate=pl.CostEstimate(
@@ -286,7 +320,7 @@
             ),
             compiler_params=pltpu.CompilerParams(vmem_limit_bytes=48 << 20),
             name="density",
-        )(ints, shards, *([] if first else sums))
+        )(*args, *([] if first else [shards, *sums]))
 
     held, fresh, ids = positions[None], positions[None], [0]
     new, sums, waves = [0], None, None

time: 40.3 us -> 36.5 us (0.906)
  starting transfers between devices: 12.2 us -> 8.9 us
  local copies, waits for them, and re-layouts: 1.56 us -> 2.83 us
  other arithmetic: 0.91 us -> 0.14 us
    ppermute x6, starting transfers between devices: 12.2 us -> 8.9 us  [swap(): return lax.ppermute(value, axis, [(i, i ^ distance) for i in range(size)])]
    unnamed x4 -> x12, local copies, waits for them, and re-layouts: 0.8 us -> 2.83 us
    concatenate x1 -> x0, other arithmetic: 0.76 us -> none  [per_device(): ints = jnp.concatenate([counts.reshape(-1), kvec_x, kvec_z, kvec_y])]
    reshape x1 -> x0, local copies, waits for them, and re-layouts: 0.76 us -> none  [per_device(): ints = jnp.concatenate([counts.reshape(-1), kvec_x, kvec_z, kvec_y])]
  transfers between devices with their start and end apart: 6 -> 6, of which waited for: 4 -> 3; matrix products, arithmetic and copies ran while one was open for 4% -> 0% of each run, Pallas kernels for 26% -> 29%
where the time goes in v1:
time: 36.5 us; the launch traced here: 36.1 us
  Pallas kernels  20.3 us (56%)
  starting transfers between devices  8.9 us (24%)
  waiting for transfers between devices  3.87 us (11%)
  local copies, waits for them, and re-layouts  2.83 us (8%)
    pallas_call x4, Pallas kernels, density(): pl.pallas_call(functools.partial(density_kernel, ids, first, last, groups...  17.7 us
    ppermute x6, starting transfers between devices, swap(): return lax.ppermute(value, axis, [(i, i ^ distance) for i in range(size)])  8.9 us
    ppermute x6, waiting for transfers between devices, swap(): return lax.ppermute(value, axis, [(i, i ^ distance) for i in range(size)])  3.87 us
    unnamed x12, local copies, waits for them, and re-layouts  2.83 us
    pallas_call x1, Pallas kernels, per_device(): pl.pallas_call(functools.partial(spectrum_kernel, groups, share, chunk, n...  2.66 us
  transfers between devices with their start and end apart: 6, of which 3 were waited for; matrix products, arithmetic and copies ran while one was open for 0% of the time, Pallas kernels for 29%

profile of v1, /device:TPU:0, one launch (start us, length us, event | category | flops | bytes accessed | tf_op | source)
XLA Modules:
  0.0 36.1 jit_solution(16589354989436607812)
XLA Ops:
  0.0 4.0 %collective-permute-start = (f32[1,3,2,2048]{3,2,1,0:T(2,128)}, f32[1,3,2,2048]{3,2,1,0:T(2,128)S(1)}, u32[]{:S(2)}, u32[]{:S(2)}) collective-permute-start(f32[1,3,2,2048]{3,2,1,0:T(2,128)} %bitcast.1), channel_id=1, source_target_pairs={{0,4},{1,5},{2,6},{3,7},{4,0},{5,1},{6,2},{7,3},{8,12},{9,13},{10,... | collective-permute-start | bytes 147464 | tf_op jit(solution)/shard_map/ppermute | solution.py:271
  4.0 0.0 copy-start
  4.0 0.8 %copy-done = f32[3,2,2048]{2,1,0:T(2,128)S(1)} copy-done((f32[3,2,2048]{2,1,0:T(2,128)S(1)}, f32[3,2,2048]{2,1,0:T(2,128)}, u32[]{:S(2)}) %copy-start) | copy-done | bytes 49176
  4.9 0.0 copy-start.2
  4.9 0.7 %copy-done.2 = s32[2,8]{1,0:T(2,128)S(1)} copy-done((s32[2,8]{1,0:T(2,128)S(1)}, s32[2,8]{1,0:T(2,128)}, u32[]{:S(2)}) %copy-start.2) | copy-done | bytes 88
  5.5 0.0 copy-start.3
  5.6 0.7 %copy-done.3 = s32[128]{0:T(128)S(1)} copy-done((s32[128]{0:T(128)S(1)}, s32[128]{0:T(128)}, u32[]{:S(2)}) %copy-start.3) | copy-done | bytes 536
  6.2 0.0 copy-start.4
  6.2 0.7 %copy-done.4 = s32[8]{0:T(128)S(1)} copy-done((s32[8]{0:T(128)S(1)}, s32[8]{0:T(128)}, u32[]{:S(2)}) %copy-start.4) | copy-done | bytes 56
  6.9 0.0 copy-start.1
  6.9 0.0 copy-start.5
  6.9 2.9 %density.4 = (f32[2,256,128]{2,1,0:T(8,128)S(1)}, f32[40,128]{1,0:T(8,128)S(1)}) custom-call(s32[2,8]{1,0:T(2,128)S(1)} %copy-done.2, s32[128]{0:T(128)S(1)} %copy-done.3, s32[8]{0:T(128)S(1)} %copy-done.4, f32[1,3,2,2048]{3,2,1,0:T(2,128)S(1)} %bitcast.2), custom_call_target="tpu_custom_call" | custom-call | flops 268435456 | bytes 49152 | tf_op jit(solution)/shard_map/density/pallas_call | solution.py:312
  9.8 0.0 collective-permute-done.refs_1_
  9.8 1.9 %collective-permute-start.1 = (f32[2,3,2,2048]{3,2,1,0:T(2,128)S(1)}, f32[2,3,2,2048]{3,2,1,0:T(2,128)S(1)}, u32[]{:S(2)}, u32[]{:S(2)}) collective-permute-start(f32[2,3,2,2048]{3,2,1,0:T(2,128)S(1)} %pad_maximum_fusion.1), channel_id=1, source_target_pairs={{0,2},{1,3},{2,0},{3,1},{4,6},{5,7},{6,4},{7,5},{8,10},{9,11},{10,... | collective-permute-start | bytes 294920 | tf_op jit(solution)/shard_map/ppermute | solution.py:271
  11.8 3.0 %density.5.refs_2_ = f32[2,256,128]{2,1,0:T(8,128)S(1)} custom-call(s32[2,8]{1,0:T(2,128)S(1)} %copy-done.2, f32[1,3,2,2048]{3,2,1,0:T(2,128)S(1)} %collective-permute-done.refs_1_, f32[2,256,128]{2,1,0:T(8,128)S(1)} %get-tuple-element.19.refs_2_, f32[40,128]{1,0:T(8,128)S(1)} %get-tuple-element.20.refs_3_.refs_4_), custom_call_target="tpu_custom_call" | custom-call | flops 268435456 | bytes 49152 | tf_op jit(solution)/shard_map/density/pallas_call | solution.py:312
  14.8 0.0 collective-permute-done.1.refs_1_
  14.8 0.0 copy-done.1
  14.8 0.1 pad_maximum_fusion
  14.9 1.0 %collective-permute-start.2 = (f32[4,3,2,2048]{3,2,1,0:T(2,128)S(1)}, f32[4,3,2,2048]{3,2,1,0:T(2,128)S(1)}, u32[]{:S(2)}, u32[]{:S(2)}) collective-permute-start(f32[4,3,2,2048]{3,2,1,0:T(2,128)S(1)} %pad_maximum_fusion), channel_id=1, source_target_pairs={{0,1},{1,0},{2,3},{3,2},{4,5},{5,4},{6,7},{7,6},{8,9},{9,8},{10,11... | collective-permute-start | bytes 589832 | tf_op jit(solution)/shard_map/ppermute | solution.py:271
  15.9 4.4 %density.6.refs_3_ = f32[2,256,128]{2,1,0:T(8,128)S(1)} custom-call(s32[2,8]{1,0:T(2,128)S(1)} %copy-done.2, f32[2,3,2,2048]{3,2,1,0:T(2,128)S(1)} %collective-permute-done.1.refs_1_, f32[2,256,128]{2,1,0:T(8,128)S(1)} %density.5.refs_2_, f32[40,128]{1,0:T(8,128)S(1)} %get-tuple-element.20.refs_3_.refs_4_), custom_call_target="tpu_custom_call" | custom-call | flops 536870912 | bytes 98304 | tf_op jit(solution)/shard_map/density/pallas_call | solution.py:312
  20.4 0.3 collective-permute-done.2.refs_2_
  20.6 0.0 copy-done.5
  20.6 7.3 %density.7 = (f32[128,128]{1,0:T(8,128)S(1)}, f32[128,128]{1,0:T(8,128)S(1)}, f32[128,128]{1,0:T(8,128)S(1)}, f32[128,128]{1,0:T(8,128)S(1)}) custom-call(s32[2,8]{1,0:T(2,128)S(1)} %copy-done.2, s32[128]{0:T(128)S(1)} %copy-done.5, f32[4,3,2,2048]{3,2,1,0:T(2,128)S(1)} %collective-permute-done.2.refs_2_, f32[2,256,128]{2,1,0:T(8,128)S(1)} %density.6.refs_3_, ...), custom_call_target="tpu_custom_call" | custom-call | flops 1073741824 | bytes 196608 | tf_op jit(solution)/shard_map/density/pallas_call | solution.py:312
  27.9 0.1 collective-permute-start.3
  28.0 0.6 %collective-permute-start.4 = (f32[128,128]{1,0:T(8,128)S(1)}, f32[128,128]{1,0:T(8,128)S(1)}, u32[]{:S(2)}, u32[]{:S(2)}) collective-permute-start(f32[128,128]{1,0:T(8,128)S(1)} %get-tuple-element.27), channel_id=1, source_target_pairs={{0,16},{8,24},{16,0},{24,8},{1,17},{9,25},{17,1},{25,9},{2,18},{10... | collective-permute-start | bytes 196616 | tf_op jit(solution)/shard_map/ppermute | solution.py:271
  28.7 1.2 %collective-permute-start.5 = (f32[128,128]{1,0:T(8,128)S(1)}, f32[128,128]{1,0:T(8,128)S(1)}, u32[]{:S(2)}, u32[]{:S(2)}) collective-permute-start(f32[128,128]{1,0:T(8,128)S(1)} %get-tuple-element.28), channel_id=1, source_target_pairs={{0,24},{8,16},{16,8},{24,0},{1,25},{9,17},{17,9},{25,1},{2,26},{10... | collective-permute-start | bytes 196616 | tf_op jit(solution)/shard_map/ppermute | solution.py:271
  29.9 0.0 collective-permute-done.3.refs_1_
  29.9 3.1 %collective-permute-done.4.refs_2_ = f32[128,128]{1,0:T(8,128)S(1)} collective-permute-done((f32[128,128]{1,0:T(8,128)S(1)}, f32[128,128]{1,0:T(8,128)S(1)}, u32[]{:S(2)}, u32[]{:S(2)}) %collective-permute-start.4) | collective-permute-done | bytes 65568 | tf_op jit(solution)/shard_map/ppermute | solution.py:271
  33.0 0.5 %collective-permute-done.5.refs_3_ = f32[128,128]{1,0:T(8,128)S(1)} collective-permute-done((f32[128,128]{1,0:T(8,128)S(1)}, f32[128,128]{1,0:T(8,128)S(1)}, u32[]{:S(2)}, u32[]{:S(2)}) %collective-permute-start.5) | collective-permute-done | bytes 65568 | tf_op jit(solution)/shard_map/ppermute | solution.py:271
  33.5 2.7 %spectrum.1 = f32[16,32,8,128]{3,2,1,0:T(8,128)} custom-call(f32[128,128]{1,0:T(8,128)S(1)} %get-tuple-element.25.refs_0_, f32[128,128]{1,0:T(8,128)S(1)} %collective-permute-done.3.refs_1_, f32[128,128]{1,0:T(8,128)S(1)} %collective-permute-done.4.refs_2_, f32[128,128]{1,0:T(8,128)S(1)} %collective-permute-done.5.refs_3_), custom_call_target="tpu_custom_call" | custom-call | tf_op jit(solution)/shard_map/spectrum/pallas_call | solution.py:344
  (1 shorter events, 0.0 us)
Async XLA Ops:
  0.0 9.8 %collective-permute-start = (f32[1,3,2,2048]{3,2,1,0:T(2,128)}, f32[1,3,2,2048]{3,2,1,0:T(2,128)S(1)}, u32[]{:S(2)}, u32[]{:S(2)}) collective-permute-start(f32[1,3,2,2048]{3,2,1,0:T(2,128)} %bitcast.1), channel_id=1, source_target_pairs={{0,4},{1,5},{2,6},{3,7},{4,0},{5,1},{6,2},{7,3},{8,12},{9,13},{10,... | collective-permute-start | bytes 147464 | tf_op jit(solution)/shard_map/ppermute | solution.py:271
  4.0 0.8 %copy-start = (f32[3,2,2048]{2,1,0:T(2,128)S(1)}, f32[3,2,2048]{2,1,0:T(2,128)}, u32[]{:S(2)}) copy-start(f32[3,2,2048]{2,1,0:T(2,128)} %param.5) | copy-start | bytes 147460
  4.9 0.7 %copy-start.2 = (s32[2,8]{1,0:T(2,128)S(1)}, s32[2,8]{1,0:T(2,128)}, u32[]{:S(2)}) copy-start(s32[2,8]{1,0:T(2,128)} %refs_0_.7) | copy-start | bytes 196
  5.5 0.7 %copy-start.3 = (s32[128]{0:T(128)S(1)}, s32[128]{0:T(128)}, u32[]{:S(2)}) copy-start(s32[128]{0:T(128)} %refs_1_.2) | copy-start | bytes 1540
  6.2 0.7 %copy-start.4 = (s32[8]{0:T(128)S(1)}, s32[8]{0:T(128)}, u32[]{:S(2)}) copy-start(s32[8]{0:T(128)} %refs_2_.1) | copy-start | bytes 100
  6.9 7.9 %copy-start.1 = (f32[3,2,2048]{2,1,0:T(2,128)S(1)}, f32[3,2,2048]{2,1,0:T(2,128)}, u32[]{:S(2)}) copy-start(f32[3,2,2048]{2,1,0:T(2,128)} %param.5) | copy-start | bytes 147460
  6.9 13.8 %copy-start.5 = (s32[128]{0:T(128)S(1)}, s32[128]{0:T(128)}, u32[]{:S(2)}) copy-start(s32[128]{0:T(128)} %refs_1_.3) | copy-start | bytes 1540
  9.8 4.9 %collective-permute-start.1 = (f32[2,3,2,2048]{3,2,1,0:T(2,128)S(1)}, f32[2,3,2,2048]{3,2,1,0:T(2,128)S(1)}, u32[]{:S(2)}, u32[]{:S(2)}) collective-permute-start(f32[2,3,2,2048]{3,2,1,0:T(2,128)S(1)} %pad_maximum_fusion.1), channel_id=1, source_target_pairs={{0,2},{1,3},{2,0},{3,1},{4,6},{5,7},{6,4},{7,5},{8,10},{9,11},{10,... | collective-permute-start | bytes 294920 | tf_op jit(solution)/shard_map/ppermute | solution.py:271
  14.9 5.7 %collective-permute-start.2 = (f32[4,3,2,2048]{3,2,1,0:T(2,128)S(1)}, f32[4,3,2,2048]{3,2,1,0:T(2,128)S(1)}, u32[]{:S(2)}, u32[]{:S(2)}) collective-permute-start(f32[4,3,2,2048]{3,2,1,0:T(2,128)S(1)} %pad_maximum_fusion), channel_id=1, source_target_pairs={{0,1},{1,0},{2,3},{3,2},{4,5},{5,4},{6,7},{7,6},{8,9},{9,8},{10,11... | collective-permute-start | bytes 589832 | tf_op jit(solution)/shard_map/ppermute | solution.py:271
  27.9 1.9 %collective-permute-start.3 = (f32[128,128]{1,0:T(8,128)S(1)}, f32[128,128]{1,0:T(8,128)S(1)}, u32[]{:S(2)}, u32[]{:S(2)}) collective-permute-start(f32[128,128]{1,0:T(8,128)S(1)} %get-tuple-element.26), channel_id=1, source_target_pairs={{0,8},{8,0},{16,24},{24,16},{1,9},{9,1},{17,25},{25,17},{2,10},{10... | collective-permute-start | bytes 196616 | tf_op jit(solution)/shard_map/ppermute | solution.py:271
  28.0 5.0 %collective-permute-start.4 = (f32[128,128]{1,0:T(8,128)S(1)}, f32[128,128]{1,0:T(8,128)S(1)}, u32[]{:S(2)}, u32[]{:S(2)}) collective-permute-start(f32[128,128]{1,0:T(8,128)S(1)} %get-tuple-element.27), channel_id=1, source_target_pairs={{0,16},{8,24},{16,0},{24,8},{1,17},{9,25},{17,1},{25,9},{2,18},{10... | collective-permute-start | bytes 196616 | tf_op jit(solution)/shard_map/ppermute | solution.py:271
  28.7 4.8 %collective-permute-start.5 = (f32[128,128]{1,0:T(8,128)S(1)}, f32[128,128]{1,0:T(8,128)S(1)}, u32[]{:S(2)}, u32[]{:S(2)}) collective-permute-start(f32[128,128]{1,0:T(8,128)S(1)} %get-tuple-element.28), channel_id=1, source_target_pairs={{0,24},{8,16},{16,8},{24,0},{1,25},{9,17},{17,9},{25,1},{2,26},{10... | collective-permute-start | bytes 196616 | tf_op jit(solution)/shard_map/ppermute | solution.py:271
